TPU v7x, 256 devices: a whole 4x4x8 slice. The times are simulated.
256 devices in a mesh: row: 16 (over z_hi, x, core), col: 16 (over y, z_lo).
Axes of the slice: x: 4, y: 4, z: 8 (z_hi: 2, z_lo: 4; z = z_hi * 4 + z_lo), core: 2. Of those that a mesh axis runs over, the one named last changes fastest.
Arguments:
- start_block: float32 [65536, 128], P(('row', 'col')), may hold values from -6 to 6
- block_values: float32 [16, 32, 512, 512], P('row', 'col'), may hold values from -0.125 to 0.125
- block_rows: int32 [16, 32], P('row', 'col'), may hold values from 0 to 7, as said below
- block_cols: int32 [16, 32], P('row', 'col'), may hold values from 0 to 7
- block_count: int32 [16, 16], P('row', 'col'), may hold values from 1 to 2, as said below
- center: float32 [1], replicated, may hold values from 0.5 to 1
- radius: float32 [1], replicated, may hold values from 0.8 to 1.2
Outputs:
- basis_block: float32 [65536, 128], P(('row', 'col'))
- projected: float32 [128, 128], replicated
Inputs may be any that keep to these rules, and one draw needn't show every extreme that they name: `block_rows`: block row within the tile; the used slots of one tile name distinct block positions. `block_count`: some tile holds exactly 2 used slots in every draw.
All inputs are finite; a program needn't handle non-finite values.
Results may differ from a plain program's by a relative error of at most 0.0003.
Values sent between devices are 32-bit elements; how exact they have to be, the bound alone decides.
A program may use at most 64 MiB of HBM per device.

v0:
```python
import jax
import jax.numpy as jnp
from jax import lax
from jax.sharding import PartitionSpec as P

ORDER = 65536
BS = 512


HIGHEST_PRECISION = lax.Precision.HIGHEST


def move_blocks(source, values, take_index, put_index, live_count, put_blocks, transpose):
    block_size = values.shape[-1]
    vec_width = source.shape[-1]
    picked = source.reshape(-1, block_size, vec_width)[take_index]
    pattern = "sba,sbv->sav" if transpose else "sab,sbv->sav"
    products = jnp.einsum(pattern, values, picked, precision=HIGHEST_PRECISION)
    live_mask = jnp.arange(values.shape[0]) < live_count
    onehot = ((put_index[None, :] == jnp.arange(put_blocks)[:, None]) & live_mask[None, :]).astype(
        jnp.float32
    )
    placed = jnp.einsum("ts,sav->tav", onehot, products, precision=HIGHEST_PRECISION)
    return placed.reshape(put_blocks * block_size, vec_width)


def body(start_block, block_values, block_rows, block_cols, block_count, center, radius):
    values = block_values[0]
    rows_local = block_rows[0]
    cols_local = block_cols[0]
    live_count = block_count[0, 0]
    tile_rows = ORDER // (BS * lax.axis_size("row"))
    tile_cols = ORDER // (BS * lax.axis_size("col"))
    shift = center[0]
    spread = radius[0]

    def transpose_half(vectors):
        gathered = lax.all_gather(vectors, "col", axis=0, tiled=True)
        return move_blocks(gathered, values, rows_local, cols_local, live_count, tile_cols, True)

    def column_share(partial_cols):
        return lax.psum_scatter(partial_cols, "row", scatter_dimension=0, tiled=True)

    def apply_scaled(vectors):
        partial_cols = transpose_half(vectors)
        whole_cols = lax.all_gather(column_share(partial_cols), "row", axis=0, tiled=True)
        partial_rows = move_blocks(
            whole_cols, values, cols_local, rows_local, live_count, tile_rows, False
        )
        system = lax.psum_scatter(partial_rows, "col", scatter_dimension=0, tiled=True)
        return (system - shift * vectors) / spread

    current = apply_scaled(start_block)
    following = 2.0 * apply_scaled(current) - start_block
    gram_local = jnp.dot(following.T, following, precision=HIGHEST_PRECISION)
    gram_matrix = lax.psum(gram_local, ("row", "col"))
    lower_factor = jnp.linalg.cholesky(gram_matrix)
    basis_block = jax.scipy.linalg.solve_triangular(lower_factor, following.T, lower=True).T
    image_block = column_share(transpose_half(basis_block))
    projected_local = jnp.dot(image_block.T, image_block, precision=HIGHEST_PRECISION)
    projected = lax.psum(projected_local, ("row", "col"))
    return (basis_block, projected)


def solution(mesh):
    in_specs = (
        P(("row", "col"), None),
        P("row", "col", None, None),
        P("row", "col"),
        P("row", "col"),
        P("row", "col"),
        P(),
        P(),
    )
    out_specs = (P(("row", "col"), None), P())
    return jax.shard_map(body, mesh=mesh, in_specs=in_specs, out_specs=out_specs, check_vma=False)
```

profile of v0, /device:TPU:1, one launch (start us, length us, event | category | flops | bytes accessed | tf_op | source)
XLA Modules:
  0.0 1387.2 jit_solution(1317139472388889234)
XLA Ops:
  9.3 81.8 %all-gather.6.cloned.1.call-done = f32[4096,128]{1,0:T(8,128)} async-done(((f32[256,128]{1,0:T(8,128)}), f32[4096,128]{1,0:T(8,128)}) %all-gather.6.cloned.1.call-update) | async-done | bytes 2097168 | tf_op jit(solution)/shard_map/all_gather | solution.py:38
  91.1 2.2 gather_fusion
  93.3 1.4 fusion.8
  96.3 1.7 copy.11
  98.1 93.9 %reduce-scatter.6.cloned.1.call-done = f32[256,128]{1,0:T(8,128)} async-done(((f32[4096,128]{1,0:T(8,128)}), f32[256,128]{1,0:T(8,128)}) %reduce-scatter.6.cloned.1.call-update) | async-done | bytes 131088 | tf_op jit(solution)/shard_map/reduce_scatter | solution.py:42
  192.1 64.0 %all-gather.8.cloned.1.call-done = f32[4096,128]{1,0:T(8,128)} async-done(((f32[256,128]{1,0:T(8,128)}), f32[4096,128]{1,0:T(8,128)}) %all-gather.8.cloned.1.call-update) | async-done | bytes 2097168 | tf_op jit(solution)/shard_map/all_gather | solution.py:46
  256.1 2.2 gather_fusion.1
  258.2 2.3 fusion.6
  262.2 1.7 copy.12
  265.3 76.1 %reduce-scatter.8.cloned.1.call-done = f32[256,128]{1,0:T(8,128)} async-done(((f32[4096,128]{1,0:T(8,128)}), f32[256,128]{1,0:T(8,128)}) %reduce-scatter.8.cloned.1.call-update) | async-done | bytes 131088 | tf_op jit(solution)/shard_map/reduce_scatter | solution.py:50
  341.4 1.6 subtract_divide_fusion
  343.0 84.8 %all-gather.10.cloned.1.call-done = f32[4096,128]{1,0:T(8,128)} async-done(((f32[256,128]{1,0:T(8,128)}), f32[4096,128]{1,0:T(8,128)}) %all-gather.10.cloned.1.call-update) | async-done | bytes 2097168 | tf_op jit(solution)/shard_map/all_gather | solution.py:38
  427.8 2.2 gather_fusion.2
  430.0 1.4 fusion.4
  433.0 1.7 copy.13
  434.8 93.9 %reduce-scatter.10.cloned.1.call-done = f32[256,128]{1,0:T(8,128)} async-done(((f32[4096,128]{1,0:T(8,128)}), f32[256,128]{1,0:T(8,128)}) %reduce-scatter.10.cloned.1.call-update) | async-done | bytes 131088 | tf_op jit(solution)/shard_map/reduce_scatter | solution.py:42
  529.0 63.8 %all-gather.12.cloned.1.call-done = f32[4096,128]{1,0:T(8,128)} async-done(((f32[256,128]{1,0:T(8,128)}), f32[4096,128]{1,0:T(8,128)}) %all-gather.12.cloned.1.call-update) | async-done | bytes 2097168 | tf_op jit(solution)/shard_map/all_gather | solution.py:46
  592.8 2.2 gather_fusion.3
  594.9 2.3 fusion.2
  598.9 1.7 copy.14
  600.7 76.8 %reduce-scatter.12.cloned.1.call-done = f32[256,128]{1,0:T(8,128)} async-done(((f32[4096,128]{1,0:T(8,128)}), f32[256,128]{1,0:T(8,128)}) %reduce-scatter.12.cloned.1.call-update) | async-done | bytes 131088 | tf_op jit(solution)/shard_map/reduce_scatter | solution.py:50
  679.5 253.3 %all-reduce.3.cloned.1.call-done = f32[128,128]{0,1:T(8,128)} async-done(((f32[128,128]{0,1:T(8,128)}), f32[128,128]{0,1:T(8,128)}) %all-reduce.3.cloned.1.call-update) | async-done | bytes 65552 | tf_op jit(solution)/shard_map/psum | solution.py:56
  934.6 11.7 cholesky.16
  947.7 9.8 custom-call.7
  958.7 73.5 %all-gather.14.cloned.1.call-done = f32[4096,128]{1,0:T(8,128)} async-done(((f32[256,128]{1,0:T(8,128)}), f32[4096,128]{1,0:T(8,128)}) %all-gather.14.cloned.1.call-update) | async-done | bytes 2097168 | tf_op jit(solution)/shard_map/all_gather | solution.py:38
  1032.2 2.2 gather_fusion.4
  1034.4 1.4 fusion
  1037.4 1.7 copy.17
  1039.2 93.9 %reduce-scatter.14.cloned.1.call-done = f32[256,128]{1,0:T(8,128)} async-done(((f32[4096,128]{1,0:T(8,128)}), f32[256,128]{1,0:T(8,128)}) %reduce-scatter.14.cloned.1.call-update) | async-done | bytes 131088 | tf_op jit(solution)/shard_map/reduce_scatter | solution.py:42
  1133.1 2.0 fusion.36
  1135.1 243.8 %all-reduce.5.cloned.1.call-done = f32[128,128]{1,0:T(8,128)} async-done(((f32[128,128]{1,0:T(8,128)}), f32[128,128]{1,0:T(8,128)}) %all-reduce.5.cloned.1.call-update) | async-done | bytes 65552 | tf_op jit(solution)/shard_map/psum | solution.py:61
  1378.9 1.5 copy.29
  (57 shorter events, 16.5 us)
Async XLA Ops:
  7.2 86.1 %copy-start = (f32[1,2,512,512]{3,2,1,0:T(8,128)S(1)}, f32[1,2,512,512]{3,2,1,0:T(8,128)}, u32[]{:S(2)}) copy-start(f32[1,2,512,512]{3,2,1,0:T(8,128)} %param.8) | copy-start | bytes 6291460
  7.2 83.9 %all-gather.6.cloned.1.call-start = ((), (), s32[]{:S(2)}) async-start(), calls=%async_computation.5 | async-start | bytes 2228224 | tf_op jit(solution)/shard_map/all_gather | solution.py:38
  7.9 184.1 %reduce-scatter.6.cloned.1.call-start = ((), (), s32[]{:S(2)}) async-start(), calls=%async_computation.6 | async-start | bytes 2228224 | tf_op jit(solution)/shard_map/reduce_scatter | solution.py:42
  93.2 1.6 copy-start.3
  98.0 158.0 %all-gather.8.cloned.1.call-start = ((), (), s32[]{:S(2)}) async-start(), calls=%async_computation.7 | async-start | bytes 2228224 | tf_op jit(solution)/shard_map/all_gather | solution.py:46
  192.0 149.3 %reduce-scatter.8.cloned.1.call-start = ((), (), s32[]{:S(2)}) async-start(), calls=%async_computation.8 | async-start | bytes 2228224 | tf_op jit(solution)/shard_map/reduce_scatter | solution.py:50
  258.2 2.6 copy-start.4
  263.9 77.5 %copy-start.1 = (f32[256,128]{1,0:T(8,128)S(1)}, f32[256,128]{1,0:T(8,128)}, u32[]{:S(2)}) copy-start(f32[256,128]{1,0:T(8,128)} %param.7) | copy-start | bytes 393220
  263.9 163.9 %all-gather.10.cloned.1.call-start = ((), (), s32[]{:S(2)}) async-start(), calls=%async_computation.9 | async-start | bytes 2228224 | tf_op jit(solution)/shard_map/all_gather | solution.py:38
  343.0 185.7 %reduce-scatter.10.cloned.1.call-start = ((), (), s32[]{:S(2)}) async-start(), calls=%async_computation.10 | async-start | bytes 2228224 | tf_op jit(solution)/shard_map/reduce_scatter | solution.py:42
  434.7 158.0 %all-gather.12.cloned.1.call-start = ((), (), s32[]{:S(2)}) async-start(), calls=%async_computation.11 | async-start | bytes 2228224 | tf_op jit(solution)/shard_map/all_gather | solution.py:46
  528.7 148.8 %reduce-scatter.12.cloned.1.call-start = ((), (), s32[]{:S(2)}) async-start(), calls=%async_computation.12 | async-start | bytes 2228224 | tf_op jit(solution)/shard_map/reduce_scatter | solution.py:50
  600.6 76.9 %copy-start.2 = (f32[256,128]{1,0:T(8,128)S(1)}, f32[256,128]{1,0:T(8,128)}, u32[]{:S(2)}) copy-start(f32[256,128]{1,0:T(8,128)} %reduce-scatter.8.cloned.1.call-done) | copy-start | bytes 393220
  600.6 332.2 %all-reduce.3.cloned.1.call-start = ((), (), s32[]{:S(2)}) async-start(), calls=%async_computation.13 | async-start | bytes 131072 | tf_op jit(solution)/shard_map/psum | solution.py:56
  679.5 352.7 %all-gather.14.cloned.1.call-start = ((), (), s32[]{:S(2)}) async-start(), calls=%async_computation.14 | async-start | bytes 2228224 | tf_op jit(solution)/shard_map/all_gather | solution.py:38
  958.4 174.7 %reduce-scatter.14.cloned.1.call-start = ((), (), s32[]{:S(2)}) async-start(), calls=%async_computation.15 | async-start | bytes 2228224 | tf_op jit(solution)/shard_map/reduce_scatter | solution.py:42
  1039.1 339.8 %all-reduce.5.cloned.1.call-start = ((), (), s32[]{:S(2)}) async-start(), calls=%async_computation.16 | async-start | bytes 131072 | tf_op jit(solution)/shard_map/psum | solution.py:61
Sparse Core Ops, SparseCore 0:
  9.8 81.2 all-gather.5
  98.1 93.8 reduce-scatter.5
  194.7 61.2 all-gather.7
  264.1 77.2 reduce-scatter.7
  343.6 84.1 all-gather.9
  434.8 93.8 reduce-scatter.9
  531.4 61.2 all-gather.11
  600.7 76.7 reduce-scatter.11
  683.6 249.1 all-reduce.2
  958.5 73.6 all-gather.13
  1039.2 93.7 reduce-scatter.13
  1139.0 239.8 all-reduce.4
where the time goes:
time: 1390 us
  waiting for transfers between devices  1300 us (94%)
  other arithmetic  26.9 us (2%)
  local copies, waits for them, and re-layouts  23 us (2%)
  matrix products  19.6 us (1%)
  between operations  16.4 us (1%)
    reduce_scatter x3, waiting for transfers between devices, column_share(): lax.psum_scatter(partial_cols, 'row', scatter_dimension=0, tiled=True)  282 us
    psum x1, waiting for transfers between devices, body(): gram_matrix = lax.psum(gram_local, ('row', 'col'))  253 us
    psum x1, waiting for transfers between devices, body(): projected = lax.psum(projected_local, ('row', 'col'))  244 us
    all_gather x3, waiting for transfers between devices, transpose_half(): gathered = lax.all_gather(vectors, 'col', axis=0, tiled=True)  240 us
    reduce_scatter x2, waiting for transfers between devices, apply_scaled(): lax.psum_scatter(partial_rows, 'col', scatter_dimension=0, tiled=True)  153 us
    all_gather x2, waiting for transfers between devices, apply_scaled(): lax.all_gather(column_share(partial_cols), 'row', axis=0, tiled=True)  128 us
  transfers between devices with their start and end apart: 12, of which 12 were waited for; matrix products, arithmetic and copies ran while one was open for 0% of the time, Pallas kernels for 0%

commit v1 on v0

v1 whole, which is shorter than its diff:
```python
import functools

import jax
import jax.numpy as jnp
from jax import lax
from jax.experimental import pallas as pl
from jax.experimental.pallas import tpu as pltpu
from jax.sharding import PartitionSpec as P

BS = 512
VEC = 128
R = 256
HIGHEST = lax.Precision.HIGHEST
MESH = pl.DeviceIdType.MESH
F32 = jnp.float32


def wrap(value, by, n):
    return lax.rem(value + (by + n), n)


class Place:
    def __init__(self):
        self.row, self.col = lax.axis_index("row"), lax.axis_index("col")
        self.core = lax.rem(self.row, 2)
        self.x = lax.rem(lax.div(self.row, 2), 4)
        self.zh = lax.div(self.row, 8)
        self.z = lax.rem(self.col, 4)
        self.y = lax.div(self.col, 4)

    def at(self, core=None, x=None, zh=None, y=None, z=None):
        core = self.core if core is None else core
        x = self.x if x is None else x
        zh = self.zh if zh is None else zh
        y = self.y if y is None else y
        z = self.z if z is None else z
        return (zh * 8 + x * 2 + core, y * 4 + z)

    def other_core(self):
        return self.at(core=1 - self.core)

    def other_half(self):
        return self.at(zh=1 - self.zh)

    def x_by(self, d):
        return self.at(x=wrap(self.x, d, 4))

    def y_by(self, d):
        return self.at(y=wrap(self.y, d, 4))

    def z_by(self, d):
        return self.at(z=wrap(self.z, d, 4))


class Wire:
    def __init__(self, send_sem, recv_sem):
        self.send_sem, self.recv_sem, self.open = send_sem, recv_sem, []

    def copy(self, src, dst, i, device):
        return pltpu.make_async_remote_copy(
            src_ref=src, dst_ref=dst, send_sem=self.send_sem.at[i], recv_sem=self.recv_sem.at[i],
            device_id=device, device_id_type=MESH)

    def send(self, src, dst, i, device):
        one = self.copy(src, dst, i, device)
        one.start()
        self.open.append(one)

    def recv(self, dst, i, device):
        self.copy(dst, dst, i, device).wait_recv()

    def drain(self):
        for one in self.open:
            one.wait_send()
        self.open = []


def greet(devices):
    barrier = pltpu.get_barrier_semaphore()
    for device in devices:
        pl.semaphore_signal(barrier, inc=1, device_id=device, device_id_type=MESH)
    pl.semaphore_wait(barrier, len(devices))


def col_peers(me):
    return [me.y_by(1), me.y_by(-1), me.z_by(1), me.z_by(2), me.z_by(3)]


def row_peers(me):
    return [me.other_core(), me.x_by(1), me.x_by(-1), me.other_half()]


AG_COL = 19


def col_gather(me, wire, g, base):
    h = R // 2
    yp, ym, y2 = wrap(me.y, 1, 4), wrap(me.y, -1, 4), wrap(me.y, 2, 4)
    up, down = me.y_by(1), me.y_by(-1)
    zs = [wrap(me.z, -k, 4) for k in range(4)]
    for k in (1, 3, 2):
        wire.send(g.at[me.col], g.at[me.col], base + k - 1, me.z_by(k))

    def full(k):
        s = me.y * 4 + zs[k]
        wire.send(g.at[s], g.at[s], base + 3 + k, up)
        wire.send(g.at[s], g.at[s], base + 7 + k, down)

    def forward(k):
        s = ym * 4 + zs[k]
        wire.recv(g.at[s], base + 3 + k, down)
        wire.send(g.at[s, 0:h], g.at[s, 0:h], base + 11 + k, up)
        s = yp * 4 + zs[k]
        wire.recv(g.at[s], base + 7 + k, up)
        wire.send(g.at[s, h:R], g.at[s, h:R], base + 15 + k, down)

    full(0)
    last = 0
    for k in (1, 3, 2):
        wire.recv(g.at[me.y * 4 + zs[k]], base + k - 1, me.z_by(-k))
        full(k)
        forward(last)
        last = k
    forward(last)
    for k in (0, 1, 3, 2):
        s = y2 * 4 + zs[k]
        wire.recv(g.at[s, 0:h], base + 11 + k, down)
        wire.recv(g.at[s, h:R], base + 15 + k, up)


RS_COL = 27


def col_scatter(me, wire, p, far, near, side, base):
    h = R // 2
    yp, ym, y2 = wrap(me.y, 1, 4), wrap(me.y, -1, 4), wrap(me.y, 2, 4)
    up, down = me.y_by(1), me.y_by(-1)
    zs = [wrap(me.z, k, 4) for k in range(4)]

    def start(k):
        s = y2 * 4 + zs[k]
        wire.send(p.at[s, 0:h], far.at[0, k], base + k, up)
        wire.send(p.at[s, h:R], far.at[1, k], base + 4 + k, down)

    def direct(k):
        s = yp * 4 + zs[k]
        wire.send(p.at[s, h:R], near.at[0, k, h:R], base + 8 + k, up)
        s = ym * 4 + zs[k]
        wire.send(p.at[s, 0:h], near.at[1, k, 0:h], base + 12 + k, down)

    def relay(k):
        s = yp * 4 + zs[k]
        wire.recv(far.at[0, k], base + k, down)
        far[0, k] = far[0, k] + p[s, 0:h]
        wire.send(far.at[0, k], near.at[0, k, 0:h], base + 16 + k, up)
        s = ym * 4 + zs[k]
        wire.recv(far.at[1, k], base + 4 + k, up)
        far[1, k] = far[1, k] + p[s, h:R]
        wire.send(far.at[1, k], near.at[1, k, h:R], base + 20 + k, down)

    def finish(k):
        s = me.y * 4 + zs[k]
        wire.recv(near.at[0, k, h:R], base + 8 + k, down)
        wire.recv(near.at[0, k, 0:h], base + 16 + k, down)
        wire.recv(near.at[1, k, 0:h], base + 12 + k, up)
        wire.recv(near.at[1, k, h:R], base + 20 + k, up)
        total = p[s] + near[0, k] + near[1, k]
        if k == 0:
            return total
        near[0, k] = total
        wire.send(near.at[0, k], side.at[k - 1], base + 23 + k, me.z_by(k))

    order = (2, 1, 3, 0)
    start(2)
    start(1)
    direct(2)
    relay(2)
    start(3)
    direct(1)
    relay(1)
    finish(2)
    start(0)
    direct(3)
    relay(3)
    finish(1)
    direct(0)
    relay(0)
    finish(3)
    total = finish(0)
    for k in order[:3]:
        wire.recv(side.at[k - 1], base + 23 + k, me.z_by(-k))
        total = total + side[k - 1]
    return total


RS_ROW = 11


def row_scatter(me, wire, p, pair, far, near, side, base):
    xp, xm, x2 = wrap(me.x, 1, 4), wrap(me.x, -1, 4), wrap(me.x, 2, 4)
    up, down, mate = me.x_by(1), me.x_by(-1), me.other_core()
    to = [me.x, xp, x2, xm]
    for k in (2, 1, 3, 0):
        wire.send(p.at[:, to[k], 1 - me.core], pair.at[k], base + k, mate)

    def join(k):
        wire.recv(pair.at[k], base + k, mate)
        pair[k] = pair[k] + p[:, to[k], me.core]

    join(2)
    wire.send(pair.at[2, 0], far.at[0], base + 4, up)
    wire.send(pair.at[2, 1], far.at[1], base + 5, down)
    join(1)
    wire.send(pair.at[1, 1], near.at[0, 1], base + 6, up)
    join(3)
    wire.send(pair.at[3, 0], near.at[1, 0], base + 7, down)
    join(0)
    wire.recv(far.at[0], base + 4, down)
    far[0] = far[0] + pair[1, 0]
    wire.send(far.at[0], near.at[0, 0], base + 8, up)
    wire.recv(far.at[1], base + 5, up)
    far[1] = far[1] + pair[3, 1]
    wire.send(far.at[1], near.at[1, 1], base + 9, down)
    wire.recv(near.at[0, 1], base + 6, down)
    wire.recv(near.at[1, 0], base + 7, up)
    wire.recv(near.at[0, 0], base + 8, down)
    wire.recv(near.at[1, 1], base + 9, up)
    other = 1 - me.zh
    near[0, other] = near[0, other] + near[1, other] + pair[0, other]
    wire.send(near.at[0, other], side, base + 10, me.other_half())
    total = near[0, me.zh] + near[1, me.zh] + pair[0, me.zh]
    wire.recv(side, base + 10, me.other_half())
    return total + side[...]


AG_ROW = 17


def row_gather(me, wire, g, base):
    h = R // 2
    xp, xm, x2 = wrap(me.x, 1, 4), wrap(me.x, -1, 4), wrap(me.x, 2, 4)
    up, down, mate = me.x_by(1), me.x_by(-1), me.other_core()
    half = [me.zh, 1 - me.zh]
    mine = g.at[me.zh, me.x, me.core]
    wire.send(mine, mine, base, me.other_half())

    def full(k):
        one = g.at[half[k], me.x, me.core]
        wire.send(one, one, base + 1 + k, up)
        wire.send(one, one, base + 3 + k, down)
        wire.send(one, one, base + 9 + k, mate)

    def forward(k):
        one = g.at[half[k], xm, me.core]
        wire.recv(one, base + 1 + k, down)
        part = g.at[half[k], xm, me.core, 0:h]
        wire.send(part, part, base + 5 + k, up)
        wire.send(one, one, base + 11 + k, mate)
        one = g.at[half[k], xp, me.core]
        wire.recv(one, base + 3 + k, up)
        part = g.at[half[k], xp, me.core, h:R]
        wire.send(part, part, base + 7 + k, down)
        wire.send(one, one, base + 13 + k, mate)

    def far(k):
        wire.recv(g.at[half[k], x2, me.core, 0:h], base + 5 + k, down)
        wire.recv(g.at[half[k], x2, me.core, h:R], base + 7 + k, up)
        one = g.at[half[k], x2, me.core]
        wire.send(one, one, base + 15 + k, mate)

    full(0)
    forward(0)
    wire.recv(g.at[half[1], me.x, me.core], base, me.other_half())
    full(1)
    far(0)
    forward(1)
    far(1)
    for first, where in ((9, me.x), (11, xm), (13, xp), (15, x2)):
        for k in range(2):
            wire.recv(g.at[half[k], where, 1 - me.core], base + first + k, mate)


def gather_kernel(v_ref, g_ref, send_sem, recv_sem, own_sem):
    me, wire = Place(), Wire(send_sem, recv_sem)
    own = pltpu.make_async_copy(v_ref, g_ref.at[me.col], own_sem)
    own.start()
    greet(col_peers(me))
    own.wait()
    col_gather(me, wire, g_ref, 0)
    wire.drain()


def row_sum_kernel(p_ref, g_ref, pair, far, near, side, send_sem, recv_sem):
    me, wire = Place(), Wire(send_sem, recv_sem)
    greet(row_peers(me))
    g_ref[me.zh, me.x, me.core] = row_scatter(me, wire, p_ref, pair, far, near, side, 0)
    row_gather(me, wire, g_ref, RS_ROW)
    wire.drain()


def row_scatter_kernel(p_ref, z_ref, pair, far, near, side, send_sem, recv_sem):
    me, wire = Place(), Wire(send_sem, recv_sem)
    greet(row_peers(me))
    z_ref[...] = row_scatter(me, wire, p_ref, pair, far, near, side, 0)
    wire.drain()


def col_sum_kernel(first, center, radius, p_ref, y_ref, old_ref, g_ref, new_ref, far, near, side, send_sem, recv_sem):
    me, wire = Place(), Wire(send_sem, recv_sem)
    greet(col_peers(me))
    system = col_scatter(me, wire, p_ref, far, near, side, 0)
    new = (system - center[0] * y_ref[...]) / radius[0]
    if not first:
        new = 2.0 * new - old_ref[...]
    new_ref[...] = new
    g_ref[me.col] = new
    col_gather(me, wire, g_ref, RS_COL)
    wire.drain()


def sums_kernel(a_ref, o_ref, mine, pair, xs, xsum, ys, zs, send_sem, recv_sem):
    me, wire = Place(), Wire(send_sem, recv_sem)
    mate = me.other_core()
    deep = me.zh * 4 + me.z
    zdev = [me.at(zh=lax.div(wrap(deep, d, 8), 4), z=lax.rem(wrap(deep, d, 8), 4)) for d in range(8)]
    greet([mate] + [me.x_by(d) for d in (1, 2, 3)] + [me.y_by(d) for d in (1, 2, 3)] + zdev[1:])
    wire.send(a_ref.at[1 - me.core], pair, 0, mate)
    wire.recv(pair, 0, mate)
    mine[...] = a_ref[me.core] + pair[...]
    for d in (2, 1, 3):
        wire.send(mine.at[wrap(me.x, d, 4)], xs.at[d - 1], d, me.x_by(d))
    total = mine[me.x]
    for d in (1, 3, 2):
        wire.recv(xs.at[d - 1], d, me.x_by(-d))
        total = total + xs[d - 1]
    xsum[...] = total
    for d in (2, 1, 3):
        wire.send(xsum.at[wrap(me.y, d, 4)], ys.at[d - 1], 3 + d, me.y_by(d))
    total = xsum[me.y]
    for d in (1, 3, 2):
        wire.recv(ys.at[d - 1], 3 + d, me.y_by(-d))
        total = total + ys[d - 1]
    zs[deep] = total
    for d in (4, 3, 5, 2, 6, 1, 7):
        wire.send(zs.at[deep], zs.at[deep], 6 + d, zdev[d])
    for d in (1, 7, 2, 6, 3, 5, 4):
        wire.recv(zs.at[wrap(deep, -d, 8)], 6 + d, zdev[8 - d])
    total = zs[0]
    for d in range(1, 8):
        total = total + zs[d]
    o_ref[me.core, me.x, me.y] = total
    part = o_ref.at[me.core, me.x, me.y]
    for d in (2, 1, 3):
        wire.send(part, part, 13 + d, me.y_by(d))
    for d in (1, 3, 2):
        wire.recv(o_ref.at[me.core, me.x, wrap(me.y, -d, 4)], 13 + d, me.y_by(-d))
    part = o_ref.at[me.core, me.x]
    for d in (2, 1, 3):
        wire.send(part, part, 16 + d, me.x_by(d))
    for d in (1, 3, 2):
        wire.recv(o_ref.at[me.core, wrap(me.x, -d, 4)], 16 + d, me.x_by(-d))
    wire.send(o_ref.at[me.core], o_ref.at[me.core], 20, mate)
    wire.recv(o_ref.at[1 - me.core], 20, mate)
    wire.drain()


def product_kernel(transpose, take, put, count, values, g_ref, p_ref):
    p_ref[...] = jnp.zeros_like(p_ref)
    dims = (((0,), (0,)), ((), ())) if transpose else (((1,), (0,)), ((), ()))
    for s in range(2):
        got = lax.dot_general(values[s], g_ref[jnp.clip(take[s], 0, 7)], dims, precision=HIGHEST, preferred_element_type=F32)
        got = jnp.where(s < count[0], got, 0.0)
        where = jnp.clip(put[s], 0, 7)
        p_ref[where] = p_ref[where] + got


VMEM = pl.BlockSpec(memory_space=pltpu.VMEM)
SMEM = pl.BlockSpec(memory_space=pltpu.SMEM)


def buf(*dims):
    return pltpu.VMEM(dims, F32)


def out(*dims):
    return jax.ShapeDtypeStruct(dims, F32)


def sems(n):
    return [pltpu.SemaphoreType.DMA((n,)), pltpu.SemaphoreType.DMA((n,))]


def remote(kernel, ident, in_specs, outs, scratch):
    many = isinstance(outs, tuple)
    return pl.pallas_call(
        kernel, out_shape=outs, in_specs=in_specs, out_specs=(VMEM,) * len(outs) if many else VMEM, scratch_shapes=scratch,
        compiler_params=pltpu.CompilerParams(collective_id=ident, has_side_effects=True))


def row_scratch():
    return [buf(4, 2, R, VEC), buf(2, R, VEC), buf(2, 2, R, VEC), buf(R, VEC)]


def col_scratch():
    return [buf(2, 4, R // 2, VEC), buf(2, 4, R, VEC), buf(3, R, VEC)]


def gather_col(v, ident):
    return remote(gather_kernel, ident, [VMEM], out(16, R, VEC), sems(AG_COL) + [pltpu.SemaphoreType.DMA])(v)


def sum_row(p, ident):
    return remote(row_sum_kernel, ident, [VMEM], out(2, 4, 2, R, VEC), row_scratch() + sems(RS_ROW + AG_ROW))(p.reshape(2, 4, 2, R, VEC))


def scatter_row(p, ident):
    return remote(row_scatter_kernel, ident, [VMEM], out(R, VEC), row_scratch() + sems(RS_ROW))(p.reshape(2, 4, 2, R, VEC))


def sum_col(p, y, old, center, radius, first, ident):
    return remote(functools.partial(col_sum_kernel, first), ident, [SMEM, SMEM, VMEM, VMEM, VMEM],
                  (out(16, R, VEC), out(R, VEC)), col_scratch() + sems(RS_COL + AG_COL))(center, radius, p.reshape(16, R, VEC), y, old)


def sum_all(a, ident):
    scratch = [buf(4, 4, 8, VEC), buf(4, 4, 8, VEC), buf(3, 4, 8, VEC), buf(4, 8, VEC), buf(3, 8, VEC), buf(8, 8, VEC)]
    return remote(sums_kernel, ident, [VMEM], out(2, 4, 4, 8, VEC), scratch + sems(21))(a.reshape(2, 4, 4, 8, VEC)).reshape(2, VEC, VEC)


def product(transpose, values, take, put, count, g):
    return pl.pallas_call(
        functools.partial(product_kernel, transpose), out_shape=out(8, BS, VEC), in_specs=[SMEM, SMEM, SMEM, VMEM, VMEM], out_specs=VMEM,
    )(take, put, count, values, g.reshape(8, BS, VEC))


def body(start_block, block_values, block_rows, block_cols, block_count, center, radius):
    values, rows, cols, count = block_values[0], block_rows[0], block_cols[0], block_count[0]
    ident = 0
    older, newer = start_block, start_block
    whole = gather_col(start_block, ident)
    for first in (True, False):
        part = product(True, values, rows, cols, count, whole)
        middle = sum_row(part, ident + 1)
        part = product(False, values, cols, rows, count, middle)
        whole, newest = sum_col(part, newer, older, center, radius, first, ident + 2)
        older, newer = newer, newest
        ident += 2
    part = product(True, values, rows, cols, count, whole)
    image = scatter_row(part, ident + 1)
    squares = [jnp.dot(a.T, a, precision=HIGHEST) for a in (newer, image)]
    gram, inner = sum_all(jnp.stack(squares), ident + 2)
    lower = jnp.linalg.cholesky(gram)
    solved = jax.scipy.linalg.solve_triangular(lower, jnp.concatenate([newer.T, inner], axis=1), lower=True)
    basis = solved[:, :R].T
    projected = jax.scipy.linalg.solve_triangular(lower, solved[:, R:].T, lower=True)
    return basis, projected


def solution(mesh):
    in_specs = (P(("row", "col"), None), P("row", "col", None, None), P("row", "col"), P("row", "col"), P("row", "col"), P(), P())
    out_specs = (P(("row", "col"), None), P())
    return jax.shard_map(body, mesh=mesh, in_specs=in_specs, out_specs=out_specs, check_vma=False)
```

time: 1390 us -> 336 us (0.24)
  waiting for transfers between devices: 1300 us -> 0 us
  Pallas kernels: 0 us -> 304 us
  local copies, waits for them, and re-layouts: 23 us -> 1.83 us
  matrix products: 19.6 us -> 3.07 us
    psum x2 -> x0, waiting for transfers between devices: 497 us -> none  [the longest x1 253 us: body(): gram_matrix = lax.psum(gram_local, ('row', 'col'))]
    reduce_scatter x5 -> x0, waiting for transfers between devices: 435 us -> none  [the longest x3 282 us: column_share(): lax.psum_scatter(partial_cols, 'row', scatter_dimension=0, tiled=True)]
    all_gather x5 -> x0, waiting for transfers between devices: 368 us -> none  [the longest x3 240 us: transpose_half(): gathered = lax.all_gather(vectors, 'col', axis=0, tiled=True)]
    pallas_call x0 -> x12, Pallas kernels: none -> 304 us  [the longest x2 98.3 us: sum_col(): remote(functools.partial(col_sum_kernel, first), ident, [SMEM, SMEM, VMEM...]
    dot_general x12 -> x2, matrix products: 18.7 us -> 1.75 us  [body(): squares = [jnp.dot(a.T, a, precision=HIGHEST) for a in (newer, image)]]
  transfers between devices with their start and end apart: 12 -> 0, of which waited for: 12 -> 0; matrix products, arithmetic and copies ran while one was open for 0% -> 0% of each run, Pallas kernels for 0% -> 0%
where the time goes in v1:
time: 336 us; the launch traced here: 335 us
  Pallas kernels  304 us (90%)
  other arithmetic  23.5 us (7%)
    pallas_call x2, Pallas kernels, sum_col(): remote(functools.partial(col_sum_kernel, first), ident, [SMEM, SMEM, VMEM...  98.3 us
    pallas_call x2, Pallas kernels, sum_row(): remote(row_sum_kernel, ident, [VMEM], out(2, 4, 2, R, VEC), row_scratch()...  91.4 us
    pallas_call x1, Pallas kernels, sum_all(): remote(sums_kernel, ident, [VMEM], out(2, 4, 4, 8, VEC), scratch + sems(21))  29.7 us
    pallas_call x1, Pallas kernels, gather_col(): remote(gather_kernel, ident, [VMEM], out(16, R, VEC), sems(AG_COL) + [plt...  29.2 us
    pallas_call x5, Pallas kernels, product(): pl.pallas_call(functools.partial(product_kernel, transpose), out_shape=ou...  28.3 us
    pallas_call x1, Pallas kernels, scatter_row(): remote(row_scatter_kernel, ident, [VMEM], out(R, VEC), row_scratch() + se...  27.3 us
    another operation x3, other arithmetic, body(): lower = jnp.linalg.cholesky(gram)  12.4 us
    another operation x2, other arithmetic, body(): jax.scipy.linalg.solve_triangular(lower, jnp.concatenate([newer.T, inner]...  10.5 us

profile of v1, /device:TPU:1, one launch (start us, length us, event | category | flops | bytes accessed | tf_op | source)
XLA Modules:
  0.0 335.3 jit_solution(6254335051983546443)
XLA Ops:
  2.6 29.2 %shard_map.86 = f32[16,256,128]{2,1,0:T(8,128)} custom-call(f32[256,128]{1,0:T(8,128)} %old_ref.3), custom_call_target="tpu_custom_call" | custom-call | tf_op jit(solution)/shard_map/pallas_call | solution.py:409
  31.8 5.7 %shard_map.87 = f32[8,512,128]{2,1,0:T(8,128)} custom-call(s32[2]{0:T(128)} %bitcast.62, s32[2]{0:T(128)} %bitcast.67, s32[1]{0:T(128)} %bitcast.37.count, f32[2,512,512]{2,1,0:T(8,128)} %bitcast.42, f32[8,512,128]{2,1,0:T(8,128)} %bitcast.54), custom_call_target="tpu_custom_call" | custom-call | tf_op jit(solution)/shard_map/pallas_call | solution.py:431
  37.4 46.9 %shard_map.88 = f32[2,4,2,256,128]{4,3,2,1,0:T(8,128)} custom-call(f32[2,4,2,256,128]{4,3,2,1,0:T(8,128)} %bitcast.50), custom_call_target="tpu_custom_call" | custom-call | tf_op jit(solution)/shard_map/pallas_call | solution.py:413
  84.4 5.6 %shard_map.89 = f32[8,512,128]{2,1,0:T(8,128)} custom-call(s32[2]{0:T(128)} %bitcast.68, s32[2]{0:T(128)} %bitcast.63, s32[1]{0:T(128)} %bitcast.38.count, f32[2,512,512]{2,1,0:T(8,128)} %bitcast.43, f32[8,512,128]{2,1,0:T(8,128)} %bitcast.51), custom_call_target="tpu_custom_call" | custom-call | tf_op jit(solution)/shard_map/pallas_call | solution.py:431
  89.9 49.6 %shard_map.90 = (f32[16,256,128]{2,1,0:T(8,128)}, f32[256,128]{1,0:T(8,128)}) custom-call(f32[1]{0:T(128)S(6)} %copy.17.center, f32[1]{0:T(128)S(6)} %copy.18.radius, f32[16,256,128]{2,1,0:T(8,128)} %bitcast.48, f32[256,128]{1,0:T(8,128)} %old_ref.3, f32[256,128]{1,0:T(8,128)} %old_ref.3), custom_call_target="tpu_custom_call" | custom-call | tf_op jit(solution)/shard_map/pallas_call | solution.py:421
  139.6 5.7 %shard_map.91 = f32[8,512,128]{2,1,0:T(8,128)} custom-call(s32[2]{0:T(128)} %bitcast.64, s32[2]{0:T(128)} %bitcast.69, s32[1]{0:T(128)} %bitcast.39.count, f32[2,512,512]{2,1,0:T(8,128)} %bitcast.44, f32[8,512,128]{2,1,0:T(8,128)} %bitcast.56), custom_call_target="tpu_custom_call" | custom-call | tf_op jit(solution)/shard_map/pallas_call | solution.py:431
  145.3 44.5 %shard_map.92 = f32[2,4,2,256,128]{4,3,2,1,0:T(8,128)} custom-call(f32[2,4,2,256,128]{4,3,2,1,0:T(8,128)} %bitcast.52), custom_call_target="tpu_custom_call" | custom-call | tf_op jit(solution)/shard_map/pallas_call | solution.py:413
  189.8 5.6 %shard_map.93 = f32[8,512,128]{2,1,0:T(8,128)} custom-call(s32[2]{0:T(128)} %bitcast.70, s32[2]{0:T(128)} %bitcast.65, s32[1]{0:T(128)} %bitcast.40.count, f32[2,512,512]{2,1,0:T(8,128)} %bitcast.45, f32[8,512,128]{2,1,0:T(8,128)} %bitcast.53), custom_call_target="tpu_custom_call" | custom-call | tf_op jit(solution)/shard_map/pallas_call | solution.py:431
  195.3 48.7 %shard_map.94 = (f32[16,256,128]{2,1,0:T(8,128)}, f32[256,128]{1,0:T(8,128)}) custom-call(f32[1]{0:T(128)S(6)} %copy.17.center, f32[1]{0:T(128)S(6)} %copy.18.radius, f32[16,256,128]{2,1,0:T(8,128)} %bitcast.47, f32[256,128]{1,0:T(8,128)} %get-tuple-element.7.y_ref, f32[256,128]{1,0:T(8,128)} %old_ref.3), custom_call_target="tpu_custom_call" | custom-call | tf_op jit(solution)/shard_map/pallas_call | solution.py:421
  244.0 5.9 %shard_map.95 = f32[8,512,128]{2,1,0:T(8,128)} custom-call(s32[2]{0:T(128)} %bitcast.66, s32[2]{0:T(128)} %bitcast.71, s32[1]{0:T(128)} %bitcast.41.count, f32[2,512,512]{2,1,0:T(8,128)} %bitcast.46, f32[8,512,128]{2,1,0:T(8,128)} %bitcast.55), custom_call_target="tpu_custom_call" | custom-call | tf_op jit(solution)/shard_map/pallas_call | solution.py:431
  249.9 0.0 copy-start
  249.9 27.3 %shard_map.96 = f32[256,128]{1,0:T(8,128)} custom-call(f32[2,4,2,256,128]{4,3,2,1,0:T(8,128)} %bitcast.49), custom_call_target="tpu_custom_call" | custom-call | tf_op jit(solution)/shard_map/pallas_call | solution.py:417
  277.1 1.4 fusion.13
  278.5 0.0 copy-done
  278.5 0.4 fusion.12
  278.9 0.7 pad_maximum_fusion.a_ref
  279.6 29.7 %shard_map.97 = f32[2,4,4,8,128]{4,3,2,1,0:T(8,128)} custom-call(f32[2,4,4,8,128]{4,3,2,1,0:T(8,128)} %pad_maximum_fusion.a_ref), custom_call_target="tpu_custom_call" | custom-call | tf_op jit(solution)/shard_map/pallas_call | solution.py:427
  309.3 0.9 fusion.11
  310.1 0.1 copy.14
  310.2 0.1 copy.13
  310.4 11.7 %cholesky.16 = f32[128,128]{1,0:T(8,128)S(1)} custom-call(f32[128,128]{1,0:T(8,128)S(1)} %fusion.9), custom_call_target="Cholesky" | custom-call | tf_op jit(solution)/shard_map/jit(cholesky)/cholesky | solution.py:452
  322.1 0.6 compare_reduce_fusion
  322.8 0.7 fusion.4
  323.4 9.8 %custom-call.10 = f32[1,128,128]{1,2,0:T(8,128)S(1)} custom-call(f32[1,128,128]{2,1,0:T(8,128)S(1)} %fusion.4), custom_call_target="InvertDiagBlocksLowerTriangular" | custom-call | tf_op jit(solution)/shard_map/jit(_solve_triangular)/triangular_solve | solution.py:453
  333.2 0.4 fusion
  333.6 0.9 fusion.5
  334.6 0.8 copy.15
  (3 shorter events, 0.1 us)
Async XLA Ops:
  249.9 28.6 %copy-start = (f32[256,128]{1,0:T(8,128)S(1)}, f32[256,128]{1,0:T(8,128)}, u32[]{:S(2)}) copy-start(f32[256,128]{1,0:T(8,128)} %get-tuple-element.8) | copy-start | bytes 393220

commit v2 on v1

v2 whole, which is shorter than its diff:
```python
import functools

import jax
import jax.numpy as jnp
from jax import lax
from jax.experimental import pallas as pl
from jax.experimental.pallas import tpu as pltpu
from jax.sharding import PartitionSpec as P

BS = 512
VEC = 128
R = 256
STREAMS = 2
W = VEC // STREAMS
LAG = 0
HIGHEST = lax.Precision.HIGHEST
MESH = pl.DeviceIdType.MESH
F32 = jnp.float32


def wrap(value, by, n):
    return lax.rem(value + (by + n), n)


class Place:
    def __init__(self):
        self.row, self.col = lax.axis_index("row"), lax.axis_index("col")
        self.core = lax.rem(self.row, 2)
        self.x = lax.rem(lax.div(self.row, 2), 4)
        self.zh = lax.div(self.row, 8)
        self.z = lax.rem(self.col, 4)
        self.y = lax.div(self.col, 4)

    def at(self, core=None, x=None, zh=None, y=None, z=None):
        core = self.core if core is None else core
        x = self.x if x is None else x
        zh = self.zh if zh is None else zh
        y = self.y if y is None else y
        z = self.z if z is None else z
        return (zh * 8 + x * 2 + core, y * 4 + z)

    def other_core(self):
        return self.at(core=1 - self.core)

    def other_half(self):
        return self.at(zh=1 - self.zh)

    def x_by(self, d):
        return self.at(x=wrap(self.x, d, 4))

    def y_by(self, d):
        return self.at(y=wrap(self.y, d, 4))

    def z_by(self, d):
        return self.at(z=wrap(self.z, d, 4))

    def deep(self):
        deep = self.zh * 4 + self.z
        on = [wrap(deep, d, 8) for d in range(8)]
        return deep, [self.at(zh=lax.div(one, 4), z=lax.rem(one, 4)) for one in on]


class Wire:
    def __init__(self, send_sem, recv_sem):
        self.send_sem, self.recv_sem, self.open = send_sem, recv_sem, []

    def copy(self, src, dst, i, device):
        return pltpu.make_async_remote_copy(
            src_ref=src, dst_ref=dst, send_sem=self.send_sem.at[i], recv_sem=self.recv_sem.at[i],
            device_id=device, device_id_type=MESH)

    def send(self, src, dst, i, device):
        one = self.copy(src, dst, i, device)
        one.start()
        self.open.append(one)

    def recv(self, dst, i, device):
        self.copy(dst, dst, i, device).wait_recv()

    def drain(self):
        for one in self.open:
            one.wait_send()
        self.open = []


def greet(devices):
    barrier = pltpu.get_barrier_semaphore()
    for device in devices:
        pl.semaphore_signal(barrier, inc=1, device_id=device, device_id_type=MESH)
    pl.semaphore_wait(barrier, len(devices))


AG_COL = 19


def col_gather(me, wire, g, base):
    h = W // 2
    yp, ym, y2 = wrap(me.y, 1, 4), wrap(me.y, -1, 4), wrap(me.y, 2, 4)
    up, down = me.y_by(1), me.y_by(-1)
    zs = [wrap(me.z, -k, 4) for k in range(4)]
    for k in (1, 3, 2):
        wire.send(g.at[me.col], g.at[me.col], base + k - 1, me.z_by(k))

    def full(k):
        s = me.y * 4 + zs[k]
        wire.send(g.at[s], g.at[s], base + 3 + k, up)
        wire.send(g.at[s], g.at[s], base + 7 + k, down)

    def forward(k):
        s = ym * 4 + zs[k]
        wire.recv(g.at[s], base + 3 + k, down)
        wire.send(g.at[s, 0:h], g.at[s, 0:h], base + 11 + k, up)
        s = yp * 4 + zs[k]
        wire.recv(g.at[s], base + 7 + k, up)
        wire.send(g.at[s, h:W], g.at[s, h:W], base + 15 + k, down)

    full(0)
    last = 0
    for k in (1, 3, 2):
        yield
        wire.recv(g.at[me.y * 4 + zs[k]], base + k - 1, me.z_by(-k))
        full(k)
        forward(last)
        last = k
    yield
    forward(last)
    yield
    for k in (0, 1, 3, 2):
        s = y2 * 4 + zs[k]
        wire.recv(g.at[s, 0:h], base + 11 + k, down)
        wire.recv(g.at[s, h:W], base + 15 + k, up)


RS_COL = 27


def col_scatter(me, wire, p, far, near, side, total, base):
    h = W // 2
    yp, ym, y2 = wrap(me.y, 1, 4), wrap(me.y, -1, 4), wrap(me.y, 2, 4)
    up, down = me.y_by(1), me.y_by(-1)
    zs = [wrap(me.z, k, 4) for k in range(4)]

    def start(k):
        s = y2 * 4 + zs[k]
        wire.send(p.at[s, 0:h], far.at[0, k], base + k, up)
        wire.send(p.at[s, h:W], far.at[1, k], base + 4 + k, down)

    def direct(k):
        s = yp * 4 + zs[k]
        wire.send(p.at[s, h:W], near.at[0, k, h:W], base + 8 + k, up)
        s = ym * 4 + zs[k]
        wire.send(p.at[s, 0:h], near.at[1, k, 0:h], base + 12 + k, down)

    def relay(k):
        s = yp * 4 + zs[k]
        wire.recv(far.at[0, k], base + k, down)
        far[0, k] = far[0, k] + p[s, 0:h]
        wire.send(far.at[0, k], near.at[0, k, 0:h], base + 16 + k, up)
        s = ym * 4 + zs[k]
        wire.recv(far.at[1, k], base + 4 + k, up)
        far[1, k] = far[1, k] + p[s, h:W]
        wire.send(far.at[1, k], near.at[1, k, h:W], base + 20 + k, down)

    def finish(k):
        s = me.y * 4 + zs[k]
        wire.recv(near.at[0, k, h:W], base + 8 + k, down)
        wire.recv(near.at[0, k, 0:h], base + 16 + k, down)
        wire.recv(near.at[1, k, 0:h], base + 12 + k, up)
        wire.recv(near.at[1, k, h:W], base + 20 + k, up)
        near[0, k] = p[s] + near[0, k] + near[1, k]
        if k > 0:
            wire.send(near.at[0, k], side.at[k - 1], base + 23 + k, me.z_by(k))

    start(2)
    start(1)
    direct(2)
    yield
    relay(2)
    start(3)
    direct(1)
    yield
    relay(1)
    start(0)
    direct(3)
    yield
    finish(2)
    relay(3)
    direct(0)
    yield
    finish(1)
    relay(0)
    yield
    finish(3)
    yield
    finish(0)
    for k in (2, 1, 3):
        wire.recv(side.at[k - 1], base + 23 + k, me.z_by(-k))
    total[...] = near[0, 0] + side[0] + side[1] + side[2]


RS_ROW = 10


def row_scatter(me, wire, p, pair, far, near, base):
    xp, xm, x2 = wrap(me.x, 1, 4), wrap(me.x, -1, 4), wrap(me.x, 2, 4)
    up, down, mate = me.x_by(1), me.x_by(-1), me.other_core()
    to = [me.x, xp, x2, xm]
    for k in (2, 1, 3, 0):
        wire.send(p.at[:, to[k], 1 - me.core], pair.at[k], base + k, mate)

    def join(k):
        wire.recv(pair.at[k], base + k, mate)
        pair[k] = pair[k] + p[:, to[k], me.core]

    yield
    join(2)
    wire.send(pair.at[2, 0], far.at[0], base + 4, up)
    wire.send(pair.at[2, 1], far.at[1], base + 5, down)
    join(1)
    wire.send(pair.at[1, 1], near.at[0, 1], base + 6, up)
    join(3)
    wire.send(pair.at[3, 0], near.at[1, 0], base + 7, down)
    join(0)
    yield
    wire.recv(far.at[0], base + 4, down)
    far[0] = far[0] + pair[1, 0]
    wire.send(far.at[0], near.at[0, 0], base + 8, up)
    wire.recv(far.at[1], base + 5, up)
    far[1] = far[1] + pair[3, 1]
    wire.send(far.at[1], near.at[1, 1], base + 9, down)
    yield
    wire.recv(near.at[0, 1], base + 6, down)
    wire.recv(near.at[1, 0], base + 7, up)
    wire.recv(near.at[0, 0], base + 8, down)
    wire.recv(near.at[1, 1], base + 9, up)
    near[0] = near[0] + near[1] + pair[0]


AG_ROW = 16


def row_gather(me, wire, g, near, side, base):
    xp, xm, x2 = wrap(me.x, 1, 4), wrap(me.x, -1, 4), wrap(me.x, 2, 4)
    up, down, mate = me.x_by(1), me.x_by(-1), me.other_core()
    for k in range(2):
        wire.send(near.at[0, k], side.at[k], base + k, me.other_half())
    yield
    for k in range(2):
        wire.recv(side.at[k], base + k, me.other_half())
        g[k, me.x, me.core] = near[0, k] + side[k]
        one = g.at[k, me.x, me.core]
        first, second = ((up, base + 2), (down, base + 4)) if k == 0 else ((down, base + 4), (up, base + 2))
        wire.send(one, one, first[1] + k, first[0])
        wire.send(one, one, second[1] + k, second[0])
        wire.send(one, one, base + 8 + k, mate)
    yield
    one = g.at[0, xm, me.core]
    wire.recv(one, base + 2, down)
    wire.send(one, one, base + 6, up)
    wire.send(one, one, base + 10, mate)
    one = g.at[1, xp, me.core]
    wire.recv(one, base + 5, up)
    wire.send(one, one, base + 7, down)
    wire.send(one, one, base + 13, mate)
    one = g.at[1, xm, me.core]
    wire.recv(one, base + 3, down)
    wire.send(one, one, base + 11, mate)
    one = g.at[0, xp, me.core]
    wire.recv(one, base + 4, up)
    wire.send(one, one, base + 12, mate)
    yield
    one = g.at[0, x2, me.core]
    wire.recv(one, base + 6, down)
    wire.send(one, one, base + 14, mate)
    one = g.at[1, x2, me.core]
    wire.recv(one, base + 7, up)
    wire.send(one, one, base + 15, mate)
    yield
    for first, where in ((8, me.x), (10, xm), (12, xp), (14, x2)):
        for k in range(2):
            wire.recv(g.at[k, where, 1 - me.core], base + first + k, mate)


def product(transpose, values, take, put, count, load, store):
    dims = (((1,), (0,)), ((), ())) if transpose else (((1,), (1,)), ((), ()))
    got = []
    for s in range(2):
        total = None
        for h in range(2):
            part = values[s, h * R:(h + 1) * R, :] if transpose else values[s, :, h * R:(h + 1) * R]
            one = lax.dot_general(load(take[s], h), part, dims, precision=HIGHEST, preferred_element_type=F32)
            total = one if total is None else total + one
        got.append(total)
    for t in range(8):
        for h in range(2):
            chunk = jnp.where(put[0] == t, got[0][:, h * R:(h + 1) * R], 0.0)
            chunk = chunk + jnp.where(jnp.logical_and(put[1] == t, count[0] > 1), got[1][:, h * R:(h + 1) * R], 0.0)
            store(t, h, chunk)


def stream(me, wire, base, rows, cols, count, center, radius, values, v, new, image, mem):
    mem = iter(mem)

    def get(n):
        return [next(mem) for _ in range(n)]

    def by_row(g):
        return lambda b, h: g[lax.div(b, 4), lax.rem(b, 4), h]

    def by_col(g):
        return lambda b, h: g[2 * b + h]

    (g,) = get(1)
    g[me.col] = v[...]
    yield from col_gather(me, wire, g, base)
    base += AG_COL
    older, newer = v, v
    for first in (True, False):
        p, pair, far, near, side, g_row = get(6)

        def put_row(t, h, chunk):
            p[t // 4, t % 4, h] = chunk

        product(True, values, rows, cols, count, by_col(g), put_row)
        yield from row_scatter(me, wire, p, pair, far, near, base)
        yield from row_gather(me, wire, g_row, near, side, base + RS_ROW)
        base += RS_ROW + AG_ROW
        q, far, near, side, total, g = get(6)

        def put_col(t, h, chunk):
            q[2 * t + h] = chunk

        product(False, values, cols, rows, count, by_row(g_row), put_col)
        yield from col_scatter(me, wire, q, far, near, side, total, base)
        fresh = (total[...] - center[0] * newer[...]) / radius[0]
        if first:
            total[...] = fresh
            older, newer = newer, total
        else:
            fresh = 2.0 * fresh - older[...]
            new[...] = fresh
        g[me.col] = fresh
        yield from col_gather(me, wire, g, base + RS_COL)
        base += RS_COL + AG_COL
    p, pair, far, near, side = get(5)

    def put_last(t, h, chunk):
        p[t // 4, t % 4, h] = chunk

    product(True, values, rows, cols, count, by_col(g), put_last)
    yield from row_scatter(me, wire, p, pair, far, near, base)
    wire.send(near.at[0, 1 - me.zh], side, base + RS_ROW, me.other_half())
    yield
    wire.recv(side, base + RS_ROW, me.other_half())
    image[...] = near[0, me.zh] + side[...]


STREAM_SEMS = AG_COL + 2 * (RS_ROW + AG_ROW + RS_COL + AG_COL) + RS_ROW + 1
SUMS = 21


def sum_all(me, wire, a_ref, o_ref, mine, pair, xs, xsum, ys, zs, base):
    mate = me.other_core()
    deep, zdev = me.deep()
    wire.send(a_ref.at[1 - me.core], pair, base, mate)
    wire.recv(pair, base, mate)
    mine[...] = a_ref[me.core] + pair[...]
    for d in (2, 1, 3):
        wire.send(mine.at[wrap(me.x, d, 4)], xs.at[d - 1], base + d, me.x_by(d))
    for d in (1, 3, 2):
        wire.recv(xs.at[d - 1], base + d, me.x_by(-d))
    xsum[...] = mine[me.x] + xs[0] + xs[1] + xs[2]
    for d in (2, 1, 3):
        wire.send(xsum.at[wrap(me.y, d, 4)], ys.at[d - 1], base + 3 + d, me.y_by(d))
    for d in (1, 3, 2):
        wire.recv(ys.at[d - 1], base + 3 + d, me.y_by(-d))
    zs[deep] = xsum[me.y] + ys[0] + ys[1] + ys[2]
    for d in (4, 3, 5, 2, 6, 1, 7):
        wire.send(zs.at[deep], zs.at[deep], base + 6 + d, zdev[d])
    for d in (1, 7, 2, 6, 3, 5, 4):
        wire.recv(zs.at[wrap(deep, -d, 8)], base + 6 + d, zdev[8 - d])
    total = zs[0]
    for d in range(1, 8):
        total = total + zs[d]
    o_ref[me.core, me.x, me.y] = total
    part = o_ref.at[me.core, me.x, me.y]
    for d in (2, 1, 3):
        wire.send(part, part, base + 13 + d, me.y_by(d))
    for d in (1, 3, 2):
        wire.recv(o_ref.at[me.core, me.x, wrap(me.y, -d, 4)], base + 13 + d, me.y_by(-d))
    part = o_ref.at[me.core, me.x]
    for d in (2, 1, 3):
        wire.send(part, part, base + 16 + d, me.x_by(d))
    for d in (1, 3, 2):
        wire.recv(o_ref.at[me.core, wrap(me.x, -d, 4)], base + 16 + d, me.x_by(-d))
    wire.send(o_ref.at[me.core], o_ref.at[me.core], base + 20, mate)
    wire.recv(o_ref.at[1 - me.core], base + 20, mate)


def stream_scratch():
    def row(whole):
        first = [buf(2, 4, 2, W, R), buf(4, 2, W, R), buf(2, W, R), buf(2, 2, W, R)]
        return first + ([buf(2, W, R), buf(2, 4, 2, W, R)] if whole else [buf(W, R)])

    col = [buf(16, W, R), buf(2, 4, W // 2, R), buf(2, 4, W, R), buf(3, W, R), buf(W, R), buf(16, W, R)]
    return [buf(16, W, R)] + 2 * (row(True) + col) + row(False)


def whole_kernel(rows, cols, count, center, radius, values, v_ref, new_ref, o_ref, *scratch):
    me = Place()
    send_sem, recv_sem = scratch[-2:]
    image, squares, *sums = scratch[:8]
    mem = scratch[8:-2]
    wire = Wire(send_sem, recv_sem)
    each = len(mem) // STREAMS
    runs = []
    for s in range(STREAMS):
        part = slice(s * W, (s + 1) * W)
        runs.append(stream(me, wire, s * STREAM_SEMS, rows, cols, count, center, radius, values, v_ref.at[part], new_ref.at[part],
                           image.at[part], mem[s * each:(s + 1) * each]))
    deep, zdev = me.deep()
    greet([me.other_core()] + [me.x_by(d) for d in (1, 2, 3)] + [me.y_by(d) for d in (1, 2, 3)] + zdev[1:])
    done, turn = [False] * STREAMS, 0
    while not all(done):
        for s in range(STREAMS):
            if not done[s] and turn >= s * LAG:
                done[s] = next(runs[s], "end") == "end"
        turn += 1
    for i, a in enumerate((new_ref[...], image[...])):
        square = lax.dot_general(a, a, (((1,), (1,)), ((), ())), precision=HIGHEST, preferred_element_type=F32)
        squares[i] = square.reshape(4, 4, 8, VEC)
    sum_all(me, wire, squares, o_ref, *sums, STREAMS * STREAM_SEMS)
    wire.drain()


VMEM = pl.BlockSpec(memory_space=pltpu.VMEM)
SMEM = pl.BlockSpec(memory_space=pltpu.SMEM)


def buf(*dims):
    return pltpu.VMEM(dims, F32)


def out(*dims):
    return jax.ShapeDtypeStruct(dims, F32)


def whole(rows, cols, count, center, radius, values, v):
    n = STREAMS * STREAM_SEMS + SUMS
    scratch = [buf(VEC, R), buf(2, 4, 4, 8, VEC)]
    scratch += [buf(4, 4, 8, VEC), buf(4, 4, 8, VEC), buf(3, 4, 8, VEC), buf(4, 8, VEC), buf(3, 8, VEC), buf(8, 8, VEC)]
    for _ in range(STREAMS):
        scratch += stream_scratch()
    scratch += [pltpu.SemaphoreType.DMA((n,)), pltpu.SemaphoreType.DMA((n,))]
    return pl.pallas_call(
        whole_kernel, out_shape=(out(VEC, R), out(2, 4, 4, 8, VEC)), in_specs=[SMEM] * 5 + [VMEM] * 2, out_specs=(VMEM, VMEM),
        scratch_shapes=scratch, compiler_params=pltpu.CompilerParams(collective_id=0, has_side_effects=True),
    )(rows, cols, count, center, radius, values, v)


def body(start_block, block_values, block_rows, block_cols, block_count, center, radius):
    rows, cols = jnp.clip(block_rows[0], 0, 7), jnp.clip(block_cols[0], 0, 7)
    new, sums = whole(rows, cols, block_count[0], center, radius, block_values[0], start_block.T)
    gram, inner = sums.reshape(2, VEC, VEC)
    lower = jnp.linalg.cholesky(gram)
    solved = jax.scipy.linalg.solve_triangular(lower, jnp.concatenate([new, inner], axis=1), lower=True)
    basis = solved[:, :R].T
    projected = jax.scipy.linalg.solve_triangular(lower, solved[:, R:].T, lower=True)
    return basis, projected


def solution(mesh):
    in_specs = (P(("row", "col"), None), P("row", "col", None, None), P("row", "col"), P("row", "col"), P("row", "col"), P(), P())
    out_specs = (P(("row", "col"), None), P())
    return jax.shard_map(body, mesh=mesh, in_specs=in_specs, out_specs=out_specs, check_vma=False)
```

time: 336 us -> 272 us (0.81)
  Pallas kernels: 304 us -> 240 us
    pallas_call x12 -> x1, Pallas kernels: 304 us -> 240 us  [whole(): pl.pallas_call(whole_kernel, out_shape=(out(VEC, R), out(2, 4, 4, 8, VEC)...]
    another operation x3 -> x2, other arithmetic: 11.1 us -> 10.5 us  [body(): jax.scipy.linalg.solve_triangular(lower, jnp.concatenate([new, inner], ax...]
where the time goes in v2:
time: 272 us
  Pallas kernels  240 us (88%)
  other arithmetic  24.1 us (9%)
  local copies, waits for them, and re-layouts  3.39 us (1%)
    pallas_call x1, Pallas kernels, whole(): pl.pallas_call(whole_kernel, out_shape=(out(VEC, R), out(2, 4, 4, 8, VEC)...  240 us
    another operation x3, other arithmetic, body(): lower = jnp.linalg.cholesky(gram)  12.4 us
    another operation x2, other arithmetic, body(): jax.scipy.linalg.solve_triangular(lower, jnp.concatenate([new, inner], ax...  10.5 us

profile of v2, /device:TPU:1, one launch (start us, length us, event | category | flops | bytes accessed | tf_op | source)
XLA Modules:
  0.0 272.2 jit_solution(13070572745870352049)
XLA Ops:
  2.6 1.3 clamp_bitcast_fusion
  3.8 1.7 copy.13
  5.5 239.9 %shard_map.86 = (f32[128,256]{1,0:T(8,128)}, f32[2,4,4,8,128]{4,3,2,1,0:T(8,128)}) custom-call(s32[2]{0:T(128)} %get-tuple-element.13.rows, s32[2]{0:T(128)} %get-tuple-element.12.cols, s32[1]{0:T(128)} %bitcast.23.count, f32[1]{0:T(128)S(6)} %copy.17.center, f32[1]{0:T(128)S(6)} %copy.18.radius, f32[2,512,512]{2,1,0:T(8,128)} %bitcast.24, f32[128,256]{1,0:T(8,128)} %bitcast.26), custom_call_target="tpu_custom_call" | custom-call | tf_op jit(solution)/shard_map/pallas_call | solution.py:455
  245.4 0.9 fusion.11
  246.3 0.1 copy.14
  246.4 11.7 %cholesky.16 = f32[128,128]{1,0:T(8,128)S(1)} custom-call(f32[128,128]{1,0:T(8,128)S(1)} %fusion.9), custom_call_target="Cholesky" | custom-call | tf_op jit(solution)/shard_map/jit(cholesky)/cholesky | solution.py:465
  258.1 0.6 compare_reduce_fusion
  258.8 0.7 fusion.4
  259.5 9.8 %custom-call.10 = f32[1,128,128]{1,2,0:T(8,128)S(1)} custom-call(f32[1,128,128]{2,1,0:T(8,128)S(1)} %fusion.4), custom_call_target="InvertDiagBlocksLowerTriangular" | custom-call | tf_op jit(solution)/shard_map/jit(_solve_triangular)/triangular_solve | solution.py:466
  269.3 1.3 fusion
  270.5 0.9 fusion.5
  271.5 0.8 copy.15
  (3 shorter events, 0.1 us)
